TPU v7x, 32 devices: a whole 2x2x4 slice. The times are simulated.
32 devices in a mesh: seq: 4 (over y, x), dp: 2 (over core), mp: 4 (over z).
Axes of the slice: x: 2, y: 2, z: 4, core: 2. Of those that a mesh axis runs over, the one named last changes fastest.
Arguments:
- tokens: bfloat16 [8, 2048, 2048], P('dp', 'seq', 'mp'), may hold values from -6 to 6
- cotangent: bfloat16 [8, 2048, 2048], P('dp', 'seq', 'mp'), may hold values from -6 to 6
- domain_id: int32 [8], P('dp'), may hold values from 0 to 7
- domain_weight: int32 [8], replicated, may hold values from 1 to 4
- lower_level: int32 [2048], P('mp'), may hold values from 2 to 23
- norm_in: float32 [2048], P('mp'), may hold values from 0.1 to 1.9
- w_input: bfloat16 [2048, 2048], P(None, 'mp'), may hold values from -0.125 to 0.125
- w_forget: bfloat16 [2048, 2048], P(None, 'mp'), may hold values from -0.125 to 0.125
- w_gate_out: bfloat16 [2048, 2048], P(None, 'mp'), may hold values from -0.125 to 0.125
- out_gain: float32 [2048], P('mp'), may hold values from 0.1 to 1.9
- w_out: bfloat16 [2048, 2048], P('mp'), may hold values from -0.125 to 0.125
- norm_mid: float32 [2048], P('mp'), may hold values from 0.1 to 1.9
- w_gate: bfloat16 [2048, 5632], P(None, 'mp'), may hold values from -0.125 to 0.125
- w_up: bfloat16 [2048, 5632], P(None, 'mp'), may hold values from -0.125 to 0.125
- w_down: bfloat16 [5632, 2048], P('mp'), may hold values from -0.078125 to 0.078125
Outputs:
- mixed: bfloat16 [8, 2048, 2048], P('dp', 'seq', 'mp')
- grad_tokens: float32 [8, 2048, 2048], P('dp', 'seq', 'mp')
- grad_norm_in: float32 [2048], P('mp')
- grad_w_input: float32 [2048, 2048], P(None, 'mp')
- grad_w_forget: float32 [2048, 2048], P(None, 'mp')
- grad_w_gate_out: float32 [2048, 2048], P(None, 'mp')
- grad_out_gain: float32 [2048], P('mp')
- grad_w_out: float32 [2048, 2048], P('mp')
- grad_norm_mid: float32 [2048], P('mp')
- grad_w_gate: float32 [2048, 5632], P(None, 'mp')
- grad_w_up: float32 [2048, 5632], P(None, 'mp')
- grad_w_down: float32 [5632, 2048], P('mp')
All inputs are finite; a program needn't handle non-finite values.
Results may differ from a plain program's by a relative error of at most 0.0075.
The roundings to bfloat16 on the way count: a program that leaves them out, or rounds other values in their place, can miss the bound.
Values may be sent and summed in bfloat16 or wider, within the bound.
No kernel may reach another device: no remote copies, remote signals or barrier semaphores. Data moves between devices by JAX's collectives and lax.ppermute only.
A program may use at most 320 MiB of HBM per device.

v0:
```python
import jax
import jax.numpy as jnp
from jax import lax
from jax.sharding import PartitionSpec as P

EPS = 1e-06


def entering(value, axis, join, neutral, backward):
    count, mine = (lax.axis_size(axis), lax.axis_index(axis))
    pieces = jax.tree.map(lambda part: lax.all_gather(part, axis), value)
    if backward:
        pieces = jax.tree.map(lambda part: part[::-1], pieces)
        mine = count - 1 - mine
    so_far = jax.tree.map(
        lambda part, zero: jnp.full_like(part, 0) + jnp.asarray(zero, part.dtype), value, neutral
    )

    def lap(position, so_far):
        longer = join(so_far, jax.tree.map(lambda part: part[position], pieces))
        return jax.tree.map(lambda new, old: jnp.where(position < mine, new, old), longer, so_far)

    return lax.fori_loop(0, count - 1, lap, so_far)


def row_total(values):
    return lax.psum(values, "mp")


def chain_pairs(earlier, later):
    return (earlier[0] * later[0], later[0] * earlier[1] + later[1])


def swish_slope(values):
    sigma = jax.nn.sigmoid(values)
    return sigma * (1.0 + values * (1.0 - sigma))


def contract_rows(left, right):
    return lax.dot_general(
        left, right, (((0,), (0,)), ((), ())), preferred_element_type=jnp.float32
    )


def contract_last(left, right):
    return lax.dot_general(
        left, right, (((1,), (1,)), ((), ())), preferred_element_type=jnp.float32
    )


def per_device(
    tokens,
    cotangent,
    domain_id,
    domain_weight,
    lower_level,
    norm_in,
    w_input,
    w_forget,
    w_gate_out,
    out_gain,
    w_out,
    norm_mid,
    w_gate,
    w_up,
    w_down,
):
    seq_count, block_len, own_width = tokens.shape
    row_count = seq_count * block_len
    full_width = own_width * lax.axis_size("mp")
    ff_local = w_gate.shape[1]
    x_rows = tokens.astype(jnp.float32).reshape(row_count, own_width)
    scale_in = lax.rsqrt(row_total(jnp.sum(x_rows * x_rows, 1)) / full_width + EPS)[:, None]
    x_hat = x_rows * scale_in
    normed_full = lax.all_gather((x_hat * norm_in).astype(jnp.bfloat16), "mp", axis=1, tiled=True)
    w_mix = jnp.concatenate((w_input, w_forget, w_gate_out), 1)
    projected = jnp.dot(normed_full, w_mix, preferred_element_type=jnp.float32)
    in_raw = projected[:, :own_width]
    forget_raw = projected[:, own_width : 2 * own_width]
    gate_raw = projected[:, 2 * own_width :]
    lower = 1.0 - jnp.exp2(-0.5 * lower_level.astype(jnp.float32))
    forget_sig = jax.nn.sigmoid(forget_raw)
    forget = lower + (1.0 - lower) * forget_sig
    in_act = jax.nn.silu(in_raw)
    inflow = in_act * (1.0 - forget)
    forget_seq = forget.reshape(seq_count, block_len, own_width)
    decay_run, state_run = lax.associative_scan(
        chain_pairs, (forget_seq, inflow.reshape(seq_count, block_len, own_width)), axis=1
    )
    unit_decay = jnp.ones((seq_count, own_width), jnp.float32)
    zero_state = jnp.zeros((seq_count, own_width), jnp.float32)
    carried_in = entering(
        (decay_run[:, -1], state_run[:, -1]), "seq", chain_pairs, (unit_decay, zero_state), False
    )
    state_in = carried_in[1]
    state_seq = state_run + decay_run * state_in[:, None, :]
    state = state_seq.reshape(row_count, own_width)
    scale_state = lax.rsqrt(row_total(jnp.sum(state * state, 1)) / full_width + EPS)[:, None]
    state_hat = state * scale_state
    gate_act = jax.nn.silu(gate_raw)
    gated = (state_hat * out_gain * gate_act).astype(jnp.bfloat16)
    out_cols = lax.all_to_all(w_out, "mp", split_axis=1, concat_axis=0, tiled=True)
    gated_full = lax.all_gather(gated, "mp", axis=1, tiled=True)
    branch = jnp.dot(gated_full, out_cols, preferred_element_type=jnp.float32)
    resid = x_rows + branch
    scale_mid = lax.rsqrt(row_total(jnp.sum(resid * resid, 1)) / full_width + EPS)[:, None]
    resid_hat = resid * scale_mid
    second_full = lax.all_gather(
        (resid_hat * norm_mid).astype(jnp.bfloat16), "mp", axis=1, tiled=True
    )
    w_pair = jnp.concatenate((w_gate, w_up), 1)

    def glu_inner(source):
        both = jnp.dot(source, w_pair, preferred_element_type=jnp.float32)
        return (both[:, :ff_local], both[:, ff_local:])

    gate_value, up_value = glu_inner(second_full)
    hidden_act = (jax.nn.silu(gate_value) * up_value).astype(jnp.bfloat16)
    glu_term = lax.psum_scatter(
        jnp.dot(hidden_act, w_down, preferred_element_type=jnp.float32),
        "mp",
        scatter_dimension=1,
        tiled=True,
    )
    block_out = resid + glu_term
    mixed = block_out.astype(jnp.bfloat16).reshape(seq_count, block_len, own_width)
    domain_hits = domain_id[:, None] == jnp.arange(domain_weight.shape[0], dtype=jnp.int32)[None, :]
    seq_weight = jnp.sum(jnp.where(domain_hits, domain_weight[None, :], 0), 1).astype(jnp.float32)
    grad_out = (cotangent.astype(jnp.float32) * seq_weight[:, None, None]).reshape(
        row_count, own_width
    )
    grad_out_full = lax.all_gather(grad_out.astype(jnp.bfloat16), "mp", axis=1, tiled=True)
    grad_hidden = contract_last(grad_out_full, w_down)
    grad_w_down = contract_rows(hidden_act, grad_out_full)
    gate_back, up_back = glu_inner(lax.optimization_barrier(second_full))
    gate_sigma = jax.nn.sigmoid(gate_back)
    grad_gate = (
        grad_hidden * up_back * gate_sigma * (1.0 + gate_back * (1.0 - gate_sigma))
    ).astype(jnp.bfloat16)
    grad_up = (grad_hidden * gate_back * gate_sigma).astype(jnp.bfloat16)
    grad_pair = jnp.concatenate((grad_gate, grad_up), 1)
    grad_w_pair = contract_rows(second_full, grad_pair)
    grad_second = lax.psum_scatter(
        contract_last(grad_pair, w_pair), "mp", scatter_dimension=1, tiled=True
    )
    grad_norm_mid = jnp.sum(grad_second * resid_hat, 0)
    grad_mid_hat = grad_second * norm_mid
    mid_dot = row_total(jnp.sum(grad_mid_hat * resid_hat, 1))[:, None] / full_width
    grad_resid = grad_out + scale_mid * (grad_mid_hat - resid_hat * mid_dot)
    grad_resid_full = lax.all_gather(grad_resid.astype(jnp.bfloat16), "mp", axis=1, tiled=True)
    grad_w_out = contract_rows(gated, grad_resid_full)
    grad_gated = contract_last(grad_resid_full, w_out)
    grad_out_gain = jnp.sum(grad_gated * state_hat * gate_act, 0)
    grad_gate_raw = (grad_gated * state_hat * out_gain * swish_slope(gate_raw)).astype(jnp.bfloat16)
    grad_state_hat = grad_gated * out_gain * gate_act
    state_dot = row_total(jnp.sum(grad_state_hat * state_hat, 1))[:, None] / full_width
    grad_state = scale_state * (grad_state_hat - state_hat * state_dot)
    grad_state_seq = grad_state.reshape(seq_count, block_len, own_width)
    back_decay, back_run = lax.associative_scan(
        chain_pairs, (forget_seq, forget_seq * grad_state_seq), reverse=True, axis=1
    )
    carried_back = entering(
        (back_decay[:, 0], back_run[:, 0]), "seq", chain_pairs, (unit_decay, zero_state), True
    )
    later_in = carried_back[1]
    passed = back_run + back_decay * later_in[:, None, :]
    adjoint_seq = grad_state_seq + jnp.concatenate((passed[:, 1:], later_in[:, None, :]), 1)
    prev_state = jnp.concatenate((state_in[:, None, :], state_seq[:, :-1]), 1)
    adjoint = adjoint_seq.reshape(row_count, own_width)
    prev_rows = prev_state.reshape(row_count, own_width)
    grad_forget = adjoint * prev_rows - adjoint * in_act
    grad_in_raw = (adjoint * (1.0 - forget) * swish_slope(in_raw)).astype(jnp.bfloat16)
    grad_forget_raw = (grad_forget * (1.0 - lower) * forget_sig * (1.0 - forget_sig)).astype(
        jnp.bfloat16
    )
    grad_projected = jnp.concatenate((grad_in_raw, grad_forget_raw, grad_gate_raw), 1)
    grad_w_mix = contract_rows(normed_full, grad_projected)
    grad_normed = lax.psum_scatter(
        contract_last(grad_projected, w_mix), "mp", scatter_dimension=1, tiled=True
    )
    grad_norm_in = jnp.sum(grad_normed * x_hat, 0)
    grad_in_hat = grad_normed * norm_in
    in_dot = row_total(jnp.sum(grad_in_hat * x_hat, 1))[:, None] / full_width
    grad_tokens = grad_resid + scale_in * (grad_in_hat - x_hat * in_dot)
    totals = lax.psum(
        (
            grad_norm_in,
            grad_w_mix[:, :own_width],
            grad_w_mix[:, own_width : 2 * own_width],
            grad_w_mix[:, 2 * own_width :],
            grad_out_gain,
            grad_w_out,
            grad_norm_mid,
            grad_w_pair[:, :ff_local],
            grad_w_pair[:, ff_local:],
            grad_w_down,
        ),
        ("seq", "dp"),
    )
    return (
        mixed,
        grad_tokens.reshape(seq_count, block_len, own_width),
        totals[0],
        totals[1],
        totals[2],
        totals[3],
        totals[4],
        totals[5],
        totals[6],
        totals[7],
        totals[8],
        totals[9],
    )


def solution(mesh):
    in_specs = (
        P("dp", "seq", "mp"),
        P("dp", "seq", "mp"),
        P("dp"),
        P(),
        P("mp"),
        P("mp"),
        P(None, "mp"),
        P(None, "mp"),
        P(None, "mp"),
        P("mp"),
        P("mp", None),
        P("mp"),
        P(None, "mp"),
        P(None, "mp"),
        P("mp", None),
    )
    out_specs = (
        P("dp", "seq", "mp"),
        P("dp", "seq", "mp"),
        P("mp"),
        P(None, "mp"),
        P(None, "mp"),
        P(None, "mp"),
        P("mp"),
        P("mp", None),
        P("mp"),
        P(None, "mp"),
        P(None, "mp"),
        P("mp", None),
    )
    return jax.shard_map(
        per_device, mesh=mesh, in_specs=in_specs, out_specs=out_specs, check_vma=False
    )
```

profile of v0, /device:TPU:0, one launch (start us, length us, event | category | flops | bytes accessed | tf_op | source)
XLA Modules:
  0.0 3189.1 jit_solution(3619002101023223962)
XLA Ops:
  32.6 142.7 %all-gather.10.cloned.1.call-done = bf16[2048,2048]{1,0:T(8,128)(2,1)} async-done(((bf16[2048,512]{1,0:T(8,128)(2,1)}), bf16[2048,2048]{1,0:T(8,128)(2,1)}) %all-gather.10.cloned.1.call-update) | async-done | bytes 8388624 | tf_op jit(solution)/shard_map/all_gather | solution.py:75
  175.3 17.4 fusion.66
  525.9 103.7 %all_to_all.19 = bf16[512,4,512]{0,2,1:T(8,128)(2,1)} all-to-all(bf16[512,4,512]{0,2,1:T(8,128)(2,1)} %bitcast.155), channel_id=1, replica_groups=mesh['seq'=4,'dp'=2,'mp'=4] {'mp'}, dimensions={1} | all-to-all | bytes 4194304 | tf_op jit(solution)/shard_map/all_to_all | solution.py:102
  633.7 74.8 %all-gather.12.cloned.1.call-done = bf16[2048,2048]{1,0:T(8,128)(2,1)} async-done(((bf16[2048,512]{1,0:T(8,128)(2,1)}), bf16[2048,2048]{1,0:T(8,128)(2,1)}) %all-gather.12.cloned.1.call-update) | async-done | bytes 8388624 | tf_op jit(solution)/shard_map/all_gather | solution.py:103
  750.5 130.5 %all-gather.14.cloned.1.call-done = bf16[2048,2048]{1,0:T(8,128)(2,1)} async-done(((bf16[2048,512]{1,0:T(8,128)(2,1)}), bf16[2048,2048]{1,0:T(8,128)(2,1)}) %all-gather.14.cloned.1.call-update) | async-done | bytes 8388624 | tf_op jit(solution)/shard_map/all_gather | solution.py:108
  881.0 32.1 %fusion.69 = f32[2048,2816]{1,0:T(8,128)} fusion(bf16[2048,2048]{1,0:T(8,128)(2,1)} %all-gather.14.cloned.1.call-done, bf16[2048,2816]{1,0:T(8,128)(2,1)} %constant_dynamic-update-slice_fusion.3), kind=kOutput, calls=%fused_computation.224 | convolution fusion | flops 23622320128 | bytes 42991616 | tf_op jit(solution)/shard_map/dot_general | solution.py:114
  913.1 117.8 %all-gather.16.cloned.1.call-done = bf16[2048,2048]{1,0:T(8,128)(2,1)} async-done(((bf16[2048,512]{1,0:T(8,128)(2,1)}), bf16[2048,2048]{1,0:T(8,128)(2,1)}) %all-gather.16.cloned.1.call-update) | async-done | bytes 8388624 | tf_op jit(solution)/shard_map/all_gather | solution.py:132
  1030.8 24.2 fusion.4
  1055.0 32.2 %fusion.7 = f32[2048,2048]{1,0:T(8,128)} fusion(bf16[2048,2816]{1,0:T(8,128)(2,1)} %constant_dynamic-update-slice_fusion.3, bf16[2048,1408]{1,0:T(8,128)(2,1)} %get-tuple-element.281, bf16[2048,1408]{1,0:T(8,128)(2,1)} %get-tuple-element.280), kind=kOutput, calls=%fused_computation.16 | convolution fusion | flops 23645388800 | bytes 39845888 | tf_op jit(solution)/shard_map/dot_general | solution.py:46
  1087.3 30.6 fusion.67
  1124.0 19.2 fusion.68
  1143.2 222.7 %reduce-scatter.6.cloned.1.call-done = f32[2048,512]{1,0:T(8,128)} async-done(((f32[2048,2048]{1,0:T(8,128)}), f32[2048,512]{1,0:T(8,128)}) %reduce-scatter.6.cloned.1.call-update) | async-done | bytes 4194320 | tf_op jit(solution)/shard_map/reduce_scatter | solution.py:143
  1382.2 267.3 %reduce-scatter.4.cloned.1.call-done = f32[2048,512]{1,0:T(8,128)} async-done(((f32[2048,2048]{1,0:T(8,128)}), f32[2048,512]{1,0:T(8,128)}) %reduce-scatter.4.cloned.1.call-update) | async-done | bytes 4194320 | tf_op jit(solution)/shard_map/reduce_scatter | solution.py:119
  1713.4 96.8 %all-gather.18.cloned.1.call-done = bf16[2048,2048]{1,0:T(8,128)(2,1)} async-done(((bf16[2048,512]{1,0:T(8,128)(2,1)}), bf16[2048,2048]{1,0:T(8,128)(2,1)}) %all-gather.18.cloned.1.call-update) | async-done | bytes 8388624 | tf_op jit(solution)/shard_map/all_gather | solution.py:150
  2056.5 17.1 slice.755
  2155.9 32.5 %rev.14 = f32[4,512,512]{2,1,0:T(8,128)} reverse(f32[4,512,512]{2,1,0:T(8,128)} %add.592), dimensions={1} | reverse | bytes 8388608 | tf_op jit(solution)/shard_map/rev | solution.py:159
  2188.4 32.5 %rev.15 = f32[4,512,512]{2,1,0:T(8,128)} reverse(f32[4,512,512]{2,1,0:T(8,128)} %add.601), dimensions={1} | reverse | bytes 8388608 | tf_op jit(solution)/shard_map/rev | solution.py:159
  2237.2 18.9 fusion.31
  2256.1 33.2 %fusion.6 = f32[2048,2816]{1,0:T(8,128)} fusion(bf16[2048,2048]{1,0:T(8,128)(2,1)} %all-gather.14.cloned.1.call-done, bf16[2048,1408]{1,0:T(8,128)(2,1)} %get-tuple-element.281, bf16[2048,1408]{1,0:T(8,128)(2,1)} %get-tuple-element.280), kind=kOutput, calls=%fused_computation.15 | convolution fusion | flops 23645388800 | bytes 42991616 | tf_op jit(solution)/shard_map/dot_general | solution.py:40
  2289.4 17.2 fusion.59
  2306.6 19.2 fusion.71
  2325.8 17.0 fusion.30
  2362.5 172.1 %reduce-scatter.8.cloned.1.call-done = f32[2048,512]{1,0:T(8,128)} async-done(((f32[2048,2048]{1,0:T(8,128)}), f32[2048,512]{1,0:T(8,128)}) %reduce-scatter.8.cloned.1.call-update) | async-done | bytes 4194320 | tf_op jit(solution)/shard_map/reduce_scatter | solution.py:178
  2569.4 568.9 %all-reduce.76.cloned.1.call-done = (f32[2048,512]{1,0:T(8,128)}, f32[2048,512]{1,0:T(8,128)}, f32[2048,512]{1,0:T(8,128)}, f32[512,2048]{1,0:T(8,128)}, f32[204...) async-done(((f32[2048,512]{1,0:T(8,128)}, f32[2048,512]{1,0:T(8,128)}, f32[2048,512]{1,0:T(8,128)}, f32[512,2048]{1,0:T(8,128)}, f32[2048,1408]{1,0:T(8,128)}, ...) | async-done | bytes 51380240 | tf_op jit(solution)/shard_map/psum | solution.py:185
  (618 shorter events, 932.4 us)
Async XLA Ops:
  7.2 168.1 %all-gather.10.cloned.1.call-start = ((), (), s32[]{:S(2)}) async-start(), calls=%async_computation.4 | async-start | bytes 10485760 | tf_op jit(solution)/shard_map/all_gather | solution.py:75
  27.3 681.2 %all-gather.12.cloned.1.call-start = ((), (), s32[]{:S(2)}) async-start(), calls=%async_computation.5 | async-start | bytes 10485760 | tf_op jit(solution)/shard_map/all_gather | solution.py:103
  27.4 165.3 %copy-start.104 = (f32[512]{0:T(512)}, f32[512]{0:T(512)S(1)}, u32[]{:S(2)}) copy-start(f32[512]{0:T(512)S(1)} %get-tuple-element.371) | copy-start | bytes 6148
  251.4 29.6 copy-start.17
  372.6 27.7 copy-start.53
  523.3 357.7 %all-gather.14.cloned.1.call-start = ((), (), s32[]{:S(2)}) async-start(), calls=%async_computation.6 | async-start | bytes 10485760 | tf_op jit(solution)/shard_map/all_gather | solution.py:108
  525.9 182.6 %copy-start.6 = (bf16[4,512,512]{2,1,0:T(8,128)(2,1)S(1)}, bf16[4,512,512]{2,1,0:T(8,128)(2,1)}, u32[]{:S(2)}) copy-start(bf16[4,512,512]{2,1,0:T(8,128)(2,1)} %param.19) | copy-start | bytes 6291460
  733.9 296.9 %all-gather.16.cloned.1.call-start = ((), (), s32[]{:S(2)}) async-start(), calls=%async_computation.8 | async-start | bytes 10485760 | tf_op jit(solution)/shard_map/all_gather | solution.py:132
  738.5 627.4 %reduce-scatter.6.cloned.1.call-start = ((), (), s32[]{:S(2)}) async-start(), calls=%async_computation.9 | async-start | bytes 20971520 | tf_op jit(solution)/shard_map/reduce_scatter | solution.py:143
  1087.2 562.2 %reduce-scatter.4.cloned.1.call-start = ((), (), s32[]{:S(2)}) async-start(), calls=%async_computation.7 | async-start | bytes 20971520 | tf_op jit(solution)/shard_map/reduce_scatter | solution.py:119
  1143.1 222.7 %copy-start.64 = (f32[2048]{0:T(1024)S(1)}, f32[2048]{0:T(1024)}, u32[]{:S(2)}) copy-start(f32[2048]{0:T(1024)} %copy-done.63) | copy-start | bytes 24580
  1143.1 222.7 %copy-start.103 = (f32[512]{0:T(512)S(1)}, f32[512]{0:T(512)}, u32[]{:S(2)}) copy-start(f32[512]{0:T(512)} %param.30) | copy-start | bytes 6148
  1143.2 667.0 %all-gather.18.cloned.1.call-start = ((), (), s32[]{:S(2)}) async-start(), calls=%async_computation.10 | async-start | bytes 10485760 | tf_op jit(solution)/shard_map/all_gather | solution.py:150
  1659.5 875.2 %reduce-scatter.8.cloned.1.call-start = ((), (), s32[]{:S(2)}) async-start(), calls=%async_computation.11 | async-start | bytes 20971520 | tf_op jit(solution)/shard_map/reduce_scatter | solution.py:178
  1708.3 101.9 %copy-start.39 = (bf16[512,2048]{1,0:T(8,128)(2,1)S(1)}, bf16[512,2048]{1,0:T(8,128)(2,1)}, u32[]{:S(2)}) copy-start(bf16[512,2048]{1,0:T(8,128)(2,1)} %param.29) | copy-start | bytes 6291460
  1708.3 101.9 %copy-start.66 = (f32[2048]{0:T(1024)S(1)}, f32[2048]{0:T(1024)}, u32[]{:S(2)}) copy-start(f32[2048]{0:T(1024)} %copy-done.65) | copy-start | bytes 24580
  1708.3 101.9 %copy-start.107 = (f32[512]{0:T(512)S(1)}, f32[512]{0:T(512)}, u32[]{:S(2)}) copy-start(f32[512]{0:T(512)} %param.28) | copy-start | bytes 6148
  2256.1 882.2 %all-reduce.76.cloned.1.call-start = ((), (), s32[]{:S(2)}) async-start(), calls=%async_computation.12 | async-start | bytes 102760448 | tf_op jit(solution)/shard_map/psum | solution.py:185
  2289.4 36.4 %slice-start = ((s8[8388608]{0:T(1024)(128)(4,1)}), s8[4194304]{0:T(1024)(128)(4,1)S(1)}, s32[]{:S(2)}) async-start(s8[8388608]{0:T(1024)(128)(4,1)} %bitcast.195), calls=%async_computation.13 | async-start | bytes 8388608
  2362.5 172.2 %copy-start.7 = (bf16[4,512,512]{2,1,0:T(8,128)(2,1)S(1)}, bf16[4,512,512]{2,1,0:T(8,128)(2,1)}, u32[]{:S(2)}) copy-start(bf16[4,512,512]{2,1,0:T(8,128)(2,1)} %param.19) | copy-start | bytes 6291460
  2362.5 172.2 %copy-start.58 = (f32[2048]{0:T(1024)S(1)}, f32[2048]{0:T(1024)}, u32[]{:S(2)}) copy-start(f32[2048]{0:T(1024)} %copy-done.57) | copy-start | bytes 24580
  2362.5 172.2 %copy-start.101 = (f32[512]{0:T(512)S(1)}, f32[512]{0:T(512)}, u32[]{:S(2)}) copy-start(f32[512]{0:T(512)} %param.24) | copy-start | bytes 6148
  2362.5 175.1 %copy-start.108 = (f32[512]{0:T(512)S(1)}, f32[512]{0:T(512)}, u32[]{:S(2)}) copy-start(f32[512]{0:T(512)} %get-tuple-element.240) | copy-start | bytes 6148
  2362.5 175.1 %copy-start.110 = (f32[512]{0:T(512)S(1)}, f32[512]{0:T(512)}, u32[]{:S(2)}) copy-start(f32[512]{0:T(512)} %get-tuple-element.238) | copy-start | bytes 6148
  (100 other events, 1155.3 us)
Sparse Core Ops, SparseCore 0:
  27.4 147.8 all-gather.9
  523.4 185.0 all-gather.11
  734.1 146.8 all-gather.13
  883.0 147.8 all-gather.15
  1087.4 278.4 reduce-scatter.5
  1368.2 281.2 reduce-scatter.3
  1659.6 150.5 all-gather.17
  2256.2 278.4 reduce-scatter.7
  2541.7 596.4 all-reduce.75
where the time goes:
time: 3220 us; the launch traced here: 3190 us
  waiting for transfers between devices  1790 us (56%)
  local copies, waits for them, and re-layouts  679 us (21%)
  matrix products  278 us (9%)
  blocking collectives  216 us (7%)
  other arithmetic  206 us (6%)
    psum x1, waiting for transfers between devices, per_device(): lax.psum((grad_norm_in, grad_w_mix[:, :own_width], grad_w_mix[:, own_widt...  569 us
    reduce_scatter x1, waiting for transfers between devices, per_device(): lax.psum_scatter(jnp.dot(hidden_act, w_down, preferred_element_type=jnp.f...  267 us
    slice x64, local copies, waits for them, and re-layouts, per_device(): lax.associative_scan(chain_pairs, (forget_seq, forget_seq * grad_state_se...  229 us
    reduce_scatter x1, waiting for transfers between devices, per_device(): lax.psum_scatter(contract_last(grad_pair, w_pair), 'mp', scatter_dimensio...  223 us
    slice x59, local copies, waits for them, and re-layouts, per_device(): lax.associative_scan(chain_pairs, (forget_seq, inflow.reshape(seq_count,...  176 us
    reduce_scatter x1, waiting for transfers between devices, per_device(): lax.psum_scatter(contract_last(grad_projected, w_mix), 'mp', scatter_dime...  172 us
    all_gather x1, waiting for transfers between devices, per_device(): lax.all_gather((x_hat * norm_in).astype(jnp.bfloat16), 'mp', axis=1, tile...  143 us
    all_gather x1, waiting for transfers between devices, per_device(): lax.all_gather((resid_hat * norm_mid).astype(jnp.bfloat16), 'mp', axis=1,...  130 us
  transfers between devices with their start and end apart: 9, of which 9 were waited for; matrix products, arithmetic and copies ran while one was open for 9% of the time, Pallas kernels for 0%

commit v1 on v0

--- a/solution.py
+++ b/solution.py
@@ -182,7 +182,15 @@
     grad_in_hat = grad_normed * norm_in
     in_dot = row_total(jnp.sum(grad_in_hat * x_hat, 1))[:, None] / full_width
     grad_tokens = grad_resid + scale_in * (grad_in_hat - x_hat * in_dot)
-    totals = lax.psum(
+
+    def show_packet(z_in):
+        bus_axis = "seq"
+        row_axis = "dp"
+        for dd in (row_axis, bus_axis):
+            z_in = jax.lax.psum(z_in, dd)
+        return z_in
+
+    totals = show_packet(
         (
             grad_norm_in,
             grad_w_mix[:, :own_width],
@@ -194,8 +202,7 @@
             grad_w_pair[:, :ff_local],
             grad_w_pair[:, ff_local:],
             grad_w_down,
-        ),
-        ("seq", "dp"),
+        )
     )
     return (
         mixed,

time: 3220 us -> 3670 us (1.14)
  waiting for transfers between devices: 1790 us -> 2250 us
    psum x1 -> x2, waiting for transfers between devices: 569 us -> 982 us  [show_packet(): z_in = jax.lax.psum(z_in, dd)]
    reduce_scatter x1, waiting for transfers between devices: 172 us -> 284 us  [per_device(): lax.psum_scatter(contract_last(grad_projected, w_mix), 'mp', scatter_dime...]
    reduce_scatter x1, waiting for transfers between devices: 223 us -> 169 us  [per_device(): lax.psum_scatter(contract_last(grad_pair, w_pair), 'mp', scatter_dimensio...]
  transfers between devices with their start and end apart: 9 -> 10, of which waited for: 9 -> 10; matrix products, arithmetic and copies ran while one was open for 9% -> 7% of each run, Pallas kernels for 0% -> 0%
where the time goes in v1:
time: 3670 us; the launch traced here: 3640 us
  waiting for transfers between devices  2250 us (61%)
  local copies, waits for them, and re-layouts  679 us (19%)
  matrix products  279 us (8%)
  blocking collectives  214 us (6%)
  other arithmetic  206 us (6%)
    psum x2, waiting for transfers between devices, show_packet(): z_in = jax.lax.psum(z_in, dd)  982 us
    reduce_scatter x1, waiting for transfers between devices, per_device(): lax.psum_scatter(contract_last(grad_projected, w_mix), 'mp', scatter_dime...  284 us
    reduce_scatter x1, waiting for transfers between devices, per_device(): lax.psum_scatter(jnp.dot(hidden_act, w_down, preferred_element_type=jnp.f...  267 us
    slice x64, local copies, waits for them, and re-layouts, per_device(): lax.associative_scan(chain_pairs, (forget_seq, forget_seq * grad_state_se...  229 us
    slice x59, local copies, waits for them, and re-layouts, per_device(): lax.associative_scan(chain_pairs, (forget_seq, inflow.reshape(seq_count,...  176 us
    reduce_scatter x1, waiting for transfers between devices, per_device(): lax.psum_scatter(contract_last(grad_pair, w_pair), 'mp', scatter_dimensio...  169 us
    all_gather x1, waiting for transfers between devices, per_device(): lax.all_gather((x_hat * norm_in).astype(jnp.bfloat16), 'mp', axis=1, tile...  143 us
    all_gather x1, waiting for transfers between devices, per_device(): lax.all_gather((resid_hat * norm_mid).astype(jnp.bfloat16), 'mp', axis=1,...  130 us
  transfers between devices with their start and end apart: 10, of which 10 were waited for; matrix products, arithmetic and copies ran while one was open for 7% of the time, Pallas kernels for 0%

profile of v1, /device:TPU:0, one launch (start us, length us, event | category | flops | bytes accessed | tf_op | source)
XLA Modules:
  0.0 3644.7 jit_solution(17940196739189735219)
XLA Ops:
  32.8 142.5 %all-gather.10.cloned.1.call-done = bf16[2048,2048]{1,0:T(8,128)(2,1)} async-done(((bf16[2048,512]{1,0:T(8,128)(2,1)}), bf16[2048,2048]{1,0:T(8,128)(2,1)}) %all-gather.10.cloned.1.call-update) | async-done | bytes 8388624 | tf_op jit(solution)/shard_map/all_gather | solution.py:75
  175.3 17.4 fusion.66
  525.9 103.7 %all_to_all.19 = bf16[512,4,512]{0,2,1:T(8,128)(2,1)} all-to-all(bf16[512,4,512]{0,2,1:T(8,128)(2,1)} %bitcast.155), channel_id=1, replica_groups=mesh['seq'=4,'dp'=2,'mp'=4] {'mp'}, dimensions={1} | all-to-all | bytes 4194304 | tf_op jit(solution)/shard_map/all_to_all | solution.py:102
  633.7 74.8 %all-gather.12.cloned.1.call-done = bf16[2048,2048]{1,0:T(8,128)(2,1)} async-done(((bf16[2048,512]{1,0:T(8,128)(2,1)}), bf16[2048,2048]{1,0:T(8,128)(2,1)}) %all-gather.12.cloned.1.call-update) | async-done | bytes 8388624 | tf_op jit(solution)/shard_map/all_gather | solution.py:103
  750.5 130.5 %all-gather.14.cloned.1.call-done = bf16[2048,2048]{1,0:T(8,128)(2,1)} async-done(((bf16[2048,512]{1,0:T(8,128)(2,1)}), bf16[2048,2048]{1,0:T(8,128)(2,1)}) %all-gather.14.cloned.1.call-update) | async-done | bytes 8388624 | tf_op jit(solution)/shard_map/all_gather | solution.py:108
  880.9 32.1 fusion.69
  913.0 117.8 %all-gather.16.cloned.1.call-done = bf16[2048,2048]{1,0:T(8,128)(2,1)} async-done(((bf16[2048,512]{1,0:T(8,128)(2,1)}), bf16[2048,2048]{1,0:T(8,128)(2,1)}) %all-gather.16.cloned.1.call-update) | async-done | bytes 8388624 | tf_op jit(solution)/shard_map/all_gather | solution.py:132
  1030.8 24.1 fusion.4
  1054.9 32.2 fusion.7
  1087.2 30.6 fusion.67
  1123.9 19.0 fusion.68
  1196.5 169.3 %reduce-scatter.6.cloned.1.call-done = f32[2048,512]{1,0:T(8,128)} async-done(((f32[2048,2048]{1,0:T(8,128)}), f32[2048,512]{1,0:T(8,128)}) %reduce-scatter.6.cloned.1.call-update) | async-done | bytes 4194320 | tf_op jit(solution)/shard_map/reduce_scatter | solution.py:143
  1382.1 267.3 %reduce-scatter.4.cloned.1.call-done = f32[2048,512]{1,0:T(8,128)} async-done(((f32[2048,2048]{1,0:T(8,128)}), f32[2048,512]{1,0:T(8,128)}) %reduce-scatter.4.cloned.1.call-update) | async-done | bytes 4194320 | tf_op jit(solution)/shard_map/reduce_scatter | solution.py:119
  1659.5 32.5 fusion.6
  1709.0 19.3 fusion.71
  1728.3 81.8 %all-gather.18.cloned.1.call-done = bf16[2048,2048]{1,0:T(8,128)(2,1)} async-done(((bf16[2048,512]{1,0:T(8,128)(2,1)}), bf16[2048,2048]{1,0:T(8,128)(2,1)}) %all-gather.18.cloned.1.call-update) | async-done | bytes 8388624 | tf_op jit(solution)/shard_map/all_gather | solution.py:150
  2055.7 17.1 slice.755
  2155.1 32.5 rev.14
  2187.6 32.6 rev.15
  2236.5 18.4 fusion.30
  2274.6 20.3 fusion.31
  2294.9 130.3 %all-reduce.81.cloned.1.call-done = (f32[2048,512]{1,0:T(8,128)}, f32[2048,512]{1,0:T(8,128)}, f32[2048,512]{1,0:T(8,128)}, f32[512,2048]{1,0:T(8,128)}, f32[204...) async-done(((f32[2048,512]{1,0:T(8,128)}, f32[2048,512]{1,0:T(8,128)}, f32[2048,512]{1,0:T(8,128)}, f32[512,2048]{1,0:T(8,128)}, f32[2048,1408]{1,0:T(8,128)}, ...) | async-done | bytes 51380240 | tf_op jit(solution)/shard_map/psum | solution.py:190
  2425.3 283.8 %reduce-scatter.8.cloned.1.call-done = f32[2048,512]{1,0:T(8,128)} async-done(((f32[2048,2048]{1,0:T(8,128)}), f32[2048,512]{1,0:T(8,128)}) %reduce-scatter.8.cloned.1.call-update) | async-done | bytes 4194320 | tf_op jit(solution)/shard_map/reduce_scatter | solution.py:178
  2742.4 851.2 %all-reduce.79.cloned.1.call-done = (f32[2048,512]{1,0:T(8,128)}, f32[2048,512]{1,0:T(8,128)}, f32[2048,512]{1,0:T(8,128)}, f32[512,2048]{1,0:T(8,128)}, f32[204...) async-done(((f32[2048,512]{1,0:T(8,128)}, f32[2048,512]{1,0:T(8,128)}, f32[2048,512]{1,0:T(8,128)}, f32[512,2048]{1,0:T(8,128)}, f32[2048,1408]{1,0:T(8,128)}, ...) | async-done | bytes 51380240 | tf_op jit(solution)/shard_map/psum | solution.py:190
  (615 shorter events, 947.2 us)
Async XLA Ops:
  7.2 168.1 %all-gather.10.cloned.1.call-start = ((), (), s32[]{:S(2)}) async-start(), calls=%async_computation.4 | async-start | bytes 10485760 | tf_op jit(solution)/shard_map/all_gather | solution.py:75
  27.3 681.2 %all-gather.12.cloned.1.call-start = ((), (), s32[]{:S(2)}) async-start(), calls=%async_computation.5 | async-start | bytes 10485760 | tf_op jit(solution)/shard_map/all_gather | solution.py:103
  27.4 165.3 %copy-start.103 = (f32[512]{0:T(512)}, f32[512]{0:T(512)S(1)}, u32[]{:S(2)}) copy-start(f32[512]{0:T(512)S(1)} %get-tuple-element.381) | copy-start | bytes 6148
  251.4 29.6 copy-start.17
  372.5 27.7 copy-start.52
  523.3 357.6 %all-gather.14.cloned.1.call-start = ((), (), s32[]{:S(2)}) async-start(), calls=%async_computation.6 | async-start | bytes 10485760 | tf_op jit(solution)/shard_map/all_gather | solution.py:108
  525.9 182.7 %copy-start.6 = (bf16[4,512,512]{2,1,0:T(8,128)(2,1)S(1)}, bf16[4,512,512]{2,1,0:T(8,128)(2,1)}, u32[]{:S(2)}) copy-start(bf16[4,512,512]{2,1,0:T(8,128)(2,1)} %param.19) | copy-start | bytes 6291460
  733.9 296.9 %all-gather.16.cloned.1.call-start = ((), (), s32[]{:S(2)}) async-start(), calls=%async_computation.8 | async-start | bytes 10485760 | tf_op jit(solution)/shard_map/all_gather | solution.py:132
  738.5 627.3 %reduce-scatter.6.cloned.1.call-start = ((), (), s32[]{:S(2)}) async-start(), calls=%async_computation.9 | async-start | bytes 20971520 | tf_op jit(solution)/shard_map/reduce_scatter | solution.py:143
  1087.1 562.2 %reduce-scatter.4.cloned.1.call-start = ((), (), s32[]{:S(2)}) async-start(), calls=%async_computation.7 | async-start | bytes 20971520 | tf_op jit(solution)/shard_map/reduce_scatter | solution.py:119
  1142.9 667.2 %all-gather.18.cloned.1.call-start = ((), (), s32[]{:S(2)}) async-start(), calls=%async_computation.10 | async-start | bytes 10485760 | tf_op jit(solution)/shard_map/all_gather | solution.py:150
  1191.5 174.3 %copy-start.63 = (f32[2048]{0:T(1024)S(1)}, f32[2048]{0:T(1024)}, u32[]{:S(2)}) copy-start(f32[2048]{0:T(1024)} %copy-done.62) | copy-start | bytes 24580
  1191.5 174.3 %copy-start.102 = (f32[512]{0:T(512)S(1)}, f32[512]{0:T(512)}, u32[]{:S(2)}) copy-start(f32[512]{0:T(512)} %param.30) | copy-start | bytes 6148
  1659.4 765.8 %all-reduce.81.cloned.1.call-start = ((), (), s32[]{:S(2)}) async-start(), calls=%async_computation.13 | async-start | bytes 102760448 | tf_op jit(solution)/shard_map/psum | solution.py:190
  1709.0 101.1 %copy-start.39 = (bf16[512,2048]{1,0:T(8,128)(2,1)S(1)}, bf16[512,2048]{1,0:T(8,128)(2,1)}, u32[]{:S(2)}) copy-start(bf16[512,2048]{1,0:T(8,128)(2,1)} %param.29) | copy-start | bytes 6291460
  1709.0 101.1 %copy-start.65 = (f32[2048]{0:T(1024)S(1)}, f32[2048]{0:T(1024)}, u32[]{:S(2)}) copy-start(f32[2048]{0:T(1024)} %copy-done.64) | copy-start | bytes 24580
  1709.0 101.1 %copy-start.106 = (f32[512]{0:T(512)S(1)}, f32[512]{0:T(512)}, u32[]{:S(2)}) copy-start(f32[512]{0:T(512)} %param.28) | copy-start | bytes 6148
  2274.5 434.5 %reduce-scatter.8.cloned.1.call-start = ((), (), s32[]{:S(2)}) async-start(), calls=%async_computation.11 | async-start | bytes 20971520 | tf_op jit(solution)/shard_map/reduce_scatter | solution.py:178
  2294.9 1298.7 %all-reduce.79.cloned.1.call-start = ((), (), s32[]{:S(2)}) async-start(), calls=%async_computation.12 | async-start | bytes 102760448 | tf_op jit(solution)/shard_map/psum | solution.py:190
  2425.2 283.9 %copy-start.7 = (bf16[4,512,512]{2,1,0:T(8,128)(2,1)S(1)}, bf16[4,512,512]{2,1,0:T(8,128)(2,1)}, u32[]{:S(2)}) copy-start(bf16[4,512,512]{2,1,0:T(8,128)(2,1)} %param.19) | copy-start | bytes 6291460
  2425.2 283.9 %copy-start.57 = (f32[2048]{0:T(1024)S(1)}, f32[2048]{0:T(1024)}, u32[]{:S(2)}) copy-start(f32[2048]{0:T(1024)} %copy-done.56) | copy-start | bytes 24580
  2425.3 283.9 %copy-start.100 = (f32[512]{0:T(512)S(1)}, f32[512]{0:T(512)}, u32[]{:S(2)}) copy-start(f32[512]{0:T(512)} %param.24) | copy-start | bytes 6148
  2425.3 286.8 %copy-start.107 = (f32[512]{0:T(512)S(1)}, f32[512]{0:T(512)}, u32[]{:S(2)}) copy-start(f32[512]{0:T(512)} %get-tuple-element.240) | copy-start | bytes 6148
  2425.3 286.8 %copy-start.109 = (f32[512]{0:T(512)S(1)}, f32[512]{0:T(512)}, u32[]{:S(2)}) copy-start(f32[512]{0:T(512)} %get-tuple-element.238) | copy-start | bytes 6148
  (98 other events, 1106.4 us)
Sparse Core Ops, SparseCore 0:
  27.4 147.8 all-gather.9
  523.4 185.0 all-gather.11
  734.0 146.8 all-gather.13
  882.9 147.8 all-gather.15
  1087.3 278.4 reduce-scatter.5
  1368.1 281.1 reduce-scatter.3
  1659.5 150.5 all-gather.17
  2274.7 150.5 all-reduce.80
  2427.6 281.4 reduce-scatter.7
  2714.4 879.1 all-reduce.78
